TPU v7x, 32 devices: a whole 2x2x4 slice. The times are simulated.
32 devices in a mesh: groups: 2 (over x), col: 16 (over z, y, core).
Axes of the slice: x: 2, y: 2, z: 4, core: 2. Of those that a mesh axis runs over, the one named last changes fastest.
Arguments:
- features: bfloat16 [32, 8, 8192], P(('groups', 'col')), parts along dimension 0
- zone_ids: int32 [32], P(('groups', 'col')), parts along dimension 0, may hold values from 0 to 7, as said below
- golden_owner: int32 [16], P('groups'), parts along dimension 0, may hold values from 0 to 15, as said below
- defect_mask: int32 [32, 8, 128], P(('groups', 'col')), parts along dimension 0, may hold values 0 or 1
- kernels: bfloat16 [2, 576, 64], replicated, may hold values from -0.25 to 0.25
Outputs:
- score: float32 [32, 8, 128], P(('groups', 'col')), parts along dimension 0
There are 2 independent parts, one for each index of `groups`. A program takes and returns all parts, laid end to end along the dimension named above; an argument that names none is the same for every part. Nothing has to cross between parts.
Inputs may be any that keep to these rules, and one draw needn't show every extreme that they name: `zone_ids`: every zone holds at least one die. golden_owner[z] is a die of zone z.
All inputs are finite; a program needn't handle non-finite values. No bound on the sum of `defect_mask` on one device may be relied on, other than what follows from the above.
Results may differ from a plain program's by a relative error of at most 0.0039.
Values may be sent and summed in bfloat16 or wider, within the bound.
A program may use at most 64 MiB of HBM per device.

v0:
```python
import jax
import jax.numpy as jnp
from jax import lax
from jax.sharding import PartitionSpec as P

C = 64
SHIFT = 6
BOX = 5
Z = 8


def box_sum(plane):
    rows = plane.shape[0]
    cols = plane.shape[1]
    reach = BOX // 2
    padded = jnp.pad(plane, ((reach, reach), (reach, reach)))
    across = padded[0:rows]
    for offset in range(1, BOX):
        across = across + padded[offset : offset + rows]
    total = across[:, 0:cols]
    for offset in range(1, BOX):
        total = total + across[:, offset : offset + cols]
    return total


def channel_sum(values, chans):
    return jnp.sum(values.reshape(values.shape[0], -1, chans), axis=-1)


def align_golden(test_tile, golden_tile, chans):
    height, spread = test_tile.shape
    width = spread // chans
    side = 2 * SHIFT + 1
    test_f = test_tile.astype(jnp.float32)
    padded = jnp.pad(golden_tile, ((SHIFT, SHIFT), (SHIFT * chans, SHIFT * chans)))
    padded_f = padded.astype(jnp.float32)
    golden_sq = channel_sum(padded_f * padded_f, chans)
    self_energy = box_sum(channel_sum(test_f * test_f, chans))

    def row_step(carry, row_off):
        numer, denom = carry
        band = lax.dynamic_slice_in_dim(padded, row_off, height, 0).astype(jnp.float32)
        sq_band = lax.dynamic_slice_in_dim(golden_sq, row_off, height, 0)
        for col_off in range(side):
            moved = band[:, col_off * chans : col_off * chans + spread]
            cross = box_sum(channel_sum(test_f * moved, chans))
            other = box_sum(sq_band[:, col_off : col_off + width])
            expo = jnp.exp(32.0 * cross / jnp.sqrt(self_energy * other + 1e-05))
            numer = numer + jnp.repeat(expo, chans, axis=1) * moved
            denom = denom + expo
        return ((numer, denom), None)

    start = (jnp.zeros((height, spread), jnp.float32), jnp.zeros((height, width), jnp.float32))
    (numer, denom), _ = lax.scan(row_step, start, jnp.arange(side, dtype=jnp.int32))
    return numer / jnp.repeat(denom, chans, axis=1)


def conv_three(tile, kernel):
    height, width, chans = tile.shape
    padded = jnp.pad(tile, ((1, 1), (1, 1), (0, 0)))
    windows = []
    for tap in range(9):
        row_off = tap // 3
        col_off = tap % 3
        windows.append(
            padded[row_off : row_off + height, col_off : col_off + width].reshape(
                height * width, chans
            )
        )
    stacked = jnp.concatenate(windows, axis=1)
    total = jnp.dot(stacked, kernel, preferred_element_type=jnp.float32)
    return total.reshape(height, width, kernel.shape[1])


def body(features, zone_ids, golden_owner, defect_mask, kernels):
    height = features.shape[1]
    width = defect_mask.shape[2]
    my_zone = zone_ids[0]
    wanted = golden_owner[my_zone]
    piece = lax.all_gather(features, "col", axis=0, tiled=True)
    positions = jnp.arange(piece.shape[0], dtype=jnp.int32)
    chosen = jnp.where((positions == wanted)[:, None, None], piece, jnp.zeros_like(piece))
    golden = jnp.sum(chosen, axis=0, keepdims=True)
    test_tile = features[0]
    aligned = align_golden(test_tile, golden[0], C)
    residual = (
        (test_tile.astype(jnp.float32) - aligned).astype(jnp.bfloat16).reshape(height, width, C)
    )
    hidden = jax.nn.relu(conv_three(residual, kernels[0])).astype(jnp.bfloat16)
    refined = residual.astype(jnp.float32) + conv_three(hidden, kernels[1])
    energy = jnp.mean(refined * refined, axis=-1)
    masked = defect_mask[0].astype(jnp.float32)
    die_sum = jnp.sum(energy * masked)
    die_count = jnp.sum(masked)
    onehot = (jnp.arange(Z, dtype=jnp.int32) == my_zone).astype(jnp.float32)
    zone_sum, zone_count = lax.psum((onehot * die_sum, onehot * die_count), "col")
    zone_mean = zone_sum / jnp.maximum(zone_count, 1.0)
    mine = jnp.sum(onehot * zone_mean)
    return (energy / (mine + 0.01))[None]


def solution(mesh):
    in_specs = (
        P(("groups", "col"), None, None),
        P(("groups", "col")),
        P("groups"),
        P(("groups", "col"), None, None),
        P(),
    )
    out_specs = P(("groups", "col"), None, None)
    return jax.shard_map(body, mesh=mesh, in_specs=in_specs, out_specs=out_specs, check_vma=False)
```

profile of v0, /device:TPU:0, one launch (start us, length us, event | category | flops | bytes accessed | tf_op | source)
XLA Modules:
  0.0 422.0 jit_solution(12637861433031280978)
XLA Ops:
  11.4 42.3 %all-gather.2.cloned.1.call-done = bf16[16,8,8192]{2,1,0:T(8,128)(2,1)} async-done(((bf16[1,8,8192]{2,1,0:T(8,128)(2,1)}), bf16[16,8,8192]{2,1,0:T(8,128)(2,1)}) %all-gather.2.cloned.1.call-update) | async-done | bytes 2097168 | tf_op jit(solution)/shard_map/all_gather | solution.py:80
  53.7 2.0 select_reduce_fusion
  57.7 318.3 %while.15 = (s32[]{:T(128)}, f32[8,8192]{1,0:T(8,128)}, f32[8,128]{1,0:T(8,128)S(1)}, s32[13]{0:T(128)S(1)}, bf16[20,8960]{1,0:T(8,128)(2,1)}, /*index=5*/f32[8,...) while((s32[]{:T(128)}, f32[8,8192]{1,0:T(8,128)}, ...), condition=%wide.region_17.18_spmd.clone, body=%wide.region_3.17_spmd.clone.sunk | while | flops 3815698 | bytes 38420288 | solution.py:54
  61.1 1.3 slice_multiply_fusion.14
  79.7 2.4 fusion.283
  85.5 1.3 slice_multiply_fusion.14
  104.1 2.5 fusion.283
  110.0 1.3 slice_multiply_fusion.14
  128.6 2.5 fusion.283
  134.5 1.3 slice_multiply_fusion.14
  153.1 2.5 fusion.283
  159.0 1.3 slice_multiply_fusion.14
  177.6 2.5 fusion.283
  183.4 1.3 slice_multiply_fusion.14
  202.1 2.5 fusion.283
  207.9 1.3 slice_multiply_fusion.14
  226.6 2.5 fusion.283
  232.4 1.3 slice_multiply_fusion.14
  251.1 2.5 fusion.283
  256.9 1.3 slice_multiply_fusion.14
  275.6 2.5 fusion.283
  281.4 1.3 slice_multiply_fusion.14
  300.1 2.5 fusion.283
  305.9 1.3 slice_multiply_fusion.14
  324.5 2.5 fusion.283
  330.4 1.3 slice_multiply_fusion.14
  333.1 1.1 reshape.318
  349.0 2.5 fusion.283
  354.9 1.3 slice_multiply_fusion.14
  373.5 2.5 fusion.283
  380.5 1.3 fusion.234
  381.8 31.4 %all-reduce.30 = (f32[8]{0:T(128)S(1)}, f32[8]{0:T(128)S(1)}) all-reduce(f32[8]{0:T(128)S(1)} %get-tuple-element.221, f32[8]{0:T(128)S(1)} %get-tuple-element.220), channel_id=1, replica_groups=mesh['groups'=2,'col'=16] {'col'}, use_global_device_ids=true, to_apply=%region_20.21 | all-reduce | flops 16 | bytes 128 | tf_op jit(solution)/shard_map/psum | solution.py:96
  (1006 shorter events, 251.4 us)
Async XLA Ops:
  6.5 4.8 %copy-start.3 = (bf16[1,8,8192]{2,1,0:T(8,128)(2,1)S(1)}, bf16[1,8,8192]{2,1,0:T(8,128)(2,1)}, u32[]{:S(2)}) copy-start(bf16[1,8,8192]{2,1,0:T(8,128)(2,1)} %param.7) | copy-start | bytes 393220
  6.5 2.6 copy-start.7
  6.5 4.0 copy-start.6
  6.5 47.1 %all-gather.2.cloned.1.call-start = ((), (), s32[]{:S(2)}) async-start(), calls=%async_computation | async-start | bytes 2228224 | tf_op jit(solution)/shard_map/all_gather | solution.py:80
  57.7 4.7 %copy-start = (f32[8,8192]{1,0:T(8,128)}, f32[8,8192]{1,0:T(8,128)S(1)}, u32[]{:S(2)}) copy-start(f32[8,8192]{1,0:T(8,128)S(1)} %get-tuple-element.456) | copy-start | bytes 786436 | tf_op jit(solution)/shard_map/while
  79.7 2.4 copy-start.1
  82.1 4.7 %copy-start = (f32[8,8192]{1,0:T(8,128)}, f32[8,8192]{1,0:T(8,128)S(1)}, u32[]{:S(2)}) copy-start(f32[8,8192]{1,0:T(8,128)S(1)} %get-tuple-element.456) | copy-start | bytes 786436 | tf_op jit(solution)/shard_map/while
  104.1 2.5 copy-start.1
  106.6 4.7 %copy-start = (f32[8,8192]{1,0:T(8,128)}, f32[8,8192]{1,0:T(8,128)S(1)}, u32[]{:S(2)}) copy-start(f32[8,8192]{1,0:T(8,128)S(1)} %get-tuple-element.456) | copy-start | bytes 786436 | tf_op jit(solution)/shard_map/while
  128.6 2.5 copy-start.1
  131.1 4.7 %copy-start = (f32[8,8192]{1,0:T(8,128)}, f32[8,8192]{1,0:T(8,128)S(1)}, u32[]{:S(2)}) copy-start(f32[8,8192]{1,0:T(8,128)S(1)} %get-tuple-element.456) | copy-start | bytes 786436 | tf_op jit(solution)/shard_map/while
  153.1 2.5 copy-start.1
  155.6 4.7 %copy-start = (f32[8,8192]{1,0:T(8,128)}, f32[8,8192]{1,0:T(8,128)S(1)}, u32[]{:S(2)}) copy-start(f32[8,8192]{1,0:T(8,128)S(1)} %get-tuple-element.456) | copy-start | bytes 786436 | tf_op jit(solution)/shard_map/while
  177.6 2.5 copy-start.1
  180.1 4.7 %copy-start = (f32[8,8192]{1,0:T(8,128)}, f32[8,8192]{1,0:T(8,128)S(1)}, u32[]{:S(2)}) copy-start(f32[8,8192]{1,0:T(8,128)S(1)} %get-tuple-element.456) | copy-start | bytes 786436 | tf_op jit(solution)/shard_map/while
  202.1 2.5 copy-start.1
  204.6 4.7 %copy-start = (f32[8,8192]{1,0:T(8,128)}, f32[8,8192]{1,0:T(8,128)S(1)}, u32[]{:S(2)}) copy-start(f32[8,8192]{1,0:T(8,128)S(1)} %get-tuple-element.456) | copy-start | bytes 786436 | tf_op jit(solution)/shard_map/while
  226.6 2.5 copy-start.1
  229.1 4.7 %copy-start = (f32[8,8192]{1,0:T(8,128)}, f32[8,8192]{1,0:T(8,128)S(1)}, u32[]{:S(2)}) copy-start(f32[8,8192]{1,0:T(8,128)S(1)} %get-tuple-element.456) | copy-start | bytes 786436 | tf_op jit(solution)/shard_map/while
  251.1 2.5 copy-start.1
  253.6 4.7 %copy-start = (f32[8,8192]{1,0:T(8,128)}, f32[8,8192]{1,0:T(8,128)S(1)}, u32[]{:S(2)}) copy-start(f32[8,8192]{1,0:T(8,128)S(1)} %get-tuple-element.456) | copy-start | bytes 786436 | tf_op jit(solution)/shard_map/while
  275.6 2.5 copy-start.1
  278.1 4.7 %copy-start = (f32[8,8192]{1,0:T(8,128)}, f32[8,8192]{1,0:T(8,128)S(1)}, u32[]{:S(2)}) copy-start(f32[8,8192]{1,0:T(8,128)S(1)} %get-tuple-element.456) | copy-start | bytes 786436 | tf_op jit(solution)/shard_map/while
  300.1 2.5 copy-start.1
  302.6 4.7 %copy-start = (f32[8,8192]{1,0:T(8,128)}, f32[8,8192]{1,0:T(8,128)S(1)}, u32[]{:S(2)}) copy-start(f32[8,8192]{1,0:T(8,128)S(1)} %get-tuple-element.456) | copy-start | bytes 786436 | tf_op jit(solution)/shard_map/while
  324.5 2.5 copy-start.1
  327.1 4.7 %copy-start = (f32[8,8192]{1,0:T(8,128)}, f32[8,8192]{1,0:T(8,128)S(1)}, u32[]{:S(2)}) copy-start(f32[8,8192]{1,0:T(8,128)S(1)} %get-tuple-element.456) | copy-start | bytes 786436 | tf_op jit(solution)/shard_map/while
  349.0 2.5 copy-start.1
  351.6 4.7 %copy-start = (f32[8,8192]{1,0:T(8,128)}, f32[8,8192]{1,0:T(8,128)S(1)}, u32[]{:S(2)}) copy-start(f32[8,8192]{1,0:T(8,128)S(1)} %get-tuple-element.456) | copy-start | bytes 786436 | tf_op jit(solution)/shard_map/while
  373.5 2.5 copy-start.1
  376.0 1.0 copy-start.2
  376.0 1.0 copy-start.4
  (1 other events, 0.9 us)
Sparse Core Ops, SparseCore 0:
  9.5 44.0 all-gather.1
where the time goes:
time: 425 us; the launch traced here: 422 us
  local copies, waits for them, and re-layouts  179 us (42%)
  other arithmetic  125 us (29%)
  waiting for transfers between devices  43 us (10%)
  blocking collectives  31.4 us (7%)
  loops' own time  27.6 us (6%)
  between operations  15 us (4%)
    reshape x170, local copies, waits for them, and re-layouts, channel_sum(): return jnp.sum(values.reshape(values.shape[0], -1, chans), axis=-1)  73.2 us
    reshape x169, local copies, waits for them, and re-layouts, row_step(): numer = numer + jnp.repeat(expo, chans, axis=1) * moved  59 us
    all_gather x1, waiting for transfers between devices, body(): piece = lax.all_gather(features, 'col', axis=0, tiled=True)  42.3 us
    reduce_sum x171, other arithmetic, channel_sum(): return jnp.sum(values.reshape(values.shape[0], -1, chans), axis=-1)  35.9 us
    add x13, other arithmetic, row_step(): numer = numer + jnp.repeat(expo, chans, axis=1) * moved  32.5 us
    broadcast_in_dim x169, local copies, waits for them, and re-layouts, row_step(): numer = numer + jnp.repeat(expo, chans, axis=1) * moved  32.3 us
    psum x1, blocking collectives, body(): lax.psum((onehot * die_sum, onehot * die_count), 'col')  31.4 us
    another operation x1, loops' own time, align_golden(): lax.scan(row_step, start, jnp.arange(side, dtype=jnp.int32))  27.6 us
  transfers between devices with their start and end apart: 1, of which 1 were waited for; matrix products, arithmetic and copies ran while one was open for 1% of the time, Pallas kernels for 0%

commit v1 on v0

--- a/solution.py
+++ b/solution.py
@@ -7,6 +7,18 @@
 SHIFT = 6
 BOX = 5
 Z = 8
+
+
+def doubled_up(shard, axis, dim):
+    ways, here = (lax.axis_size(axis), lax.axis_index(axis))
+    grown, reach = (shard, 1)
+    while reach < ways:
+        theirs = lax.ppermute(grown, axis, [(d, d ^ reach) for d in range(ways)])
+        mine_first = jnp.concatenate([grown, theirs], axis=dim)
+        theirs_first = jnp.concatenate([theirs, grown], axis=dim)
+        grown = jnp.where(here & reach == 0, mine_first, theirs_first)
+        reach = 2 * reach
+    return grown
 
 
 def box_sum(plane):
@@ -77,7 +89,7 @@
     width = defect_mask.shape[2]
     my_zone = zone_ids[0]
     wanted = golden_owner[my_zone]
-    piece = lax.all_gather(features, "col", axis=0, tiled=True)
+    piece = doubled_up(features, "col", 0)
     positions = jnp.arange(piece.shape[0], dtype=jnp.int32)
     chosen = jnp.where((positions == wanted)[:, None, None], piece, jnp.zeros_like(piece))
     golden = jnp.sum(chosen, axis=0, keepdims=True)

time: 425 us -> 440 us (1.035)
  waiting for transfers between devices: 43 us -> 59.9 us
  between operations: 15 us -> 1.62 us
  starting transfers between devices: 0.01 us -> 7.81 us
    ppermute x0 -> x4, waiting for transfers between devices: none -> 59.9 us  [doubled_up(): theirs = lax.ppermute(grown, axis, [(d, d ^ reach) for d in range(ways)])]
    all_gather x1 -> x0, waiting for transfers between devices: 42.3 us -> none  [body(): piece = lax.all_gather(features, 'col', axis=0, tiled=True)]
    ppermute x0 -> x4, starting transfers between devices: none -> 7.81 us  [doubled_up(): theirs = lax.ppermute(grown, axis, [(d, d ^ reach) for d in range(ways)])]
  transfers between devices with their start and end apart: 1 -> 4, of which waited for: 1 -> 4; matrix products, arithmetic and copies ran while one was open for 1% -> 1% of each run, Pallas kernels for 0% -> 0%
where the time goes in v1:
time: 440 us; the launch traced here: 438 us
  local copies, waits for them, and re-layouts  180 us (41%)
  other arithmetic  125 us (28%)
  waiting for transfers between devices  59.9 us (14%)
  blocking collectives  33.1 us (8%)
  loops' own time  30 us (7%)
  starting transfers between devices  7.81 us (2%)
    reshape x170, local copies, waits for them, and re-layouts, channel_sum(): return jnp.sum(values.reshape(values.shape[0], -1, chans), axis=-1)  73.2 us
    ppermute x4, waiting for transfers between devices, doubled_up(): theirs = lax.ppermute(grown, axis, [(d, d ^ reach) for d in range(ways)])  59.9 us
    reshape x169, local copies, waits for them, and re-layouts, row_step(): numer = numer + jnp.repeat(expo, chans, axis=1) * moved  59.2 us
    reduce_sum x171, other arithmetic, channel_sum(): return jnp.sum(values.reshape(values.shape[0], -1, chans), axis=-1)  35.9 us
    psum x1, blocking collectives, body(): lax.psum((onehot * die_sum, onehot * die_count), 'col')  33.1 us
    broadcast_in_dim x169, local copies, waits for them, and re-layouts, row_step(): numer = numer + jnp.repeat(expo, chans, axis=1) * moved  32.3 us
    add x13, other arithmetic, row_step(): numer = numer + jnp.repeat(expo, chans, axis=1) * moved  32.1 us
    another operation x1, loops' own time, align_golden(): lax.scan(row_step, start, jnp.arange(side, dtype=jnp.int32))  30 us
  transfers between devices with their start and end apart: 4, of which 4 were waited for; matrix products, arithmetic and copies ran while one was open for 1% of the time, Pallas kernels for 0%

profile of v1, /device:TPU:0, one launch (start us, length us, event | category | flops | bytes accessed | tf_op | source)
XLA Modules:
  0.0 437.9 jit_solution(10875953348137278870)
XLA Ops:
  2.7 2.9 collective-permute-start.1
  8.3 3.9 collective-permute-done.1
  12.3 1.9 collective-permute-start.2
  15.7 10.2 %collective-permute-done.2 = bf16[4,8,8192]{2,1,0:T(8,128)(2,1)S(1)} collective-permute-done((bf16[4,8,8192]{2,1,0:T(8,128)(2,1)S(1)}, bf16[4,8,8192]{2,1,0:T(8,128)(2,1)S(1)}, u32[]{:S(2)}, u32[]{:S(2)}) %collective-permute-start.2) | collective-permute-done | bytes 524320 | tf_op jit(solution)/shard_map/ppermute | solution.py:16
  26.0 2.6 collective-permute-start.3
  28.6 44.7 %collective-permute-done.3 = bf16[8,8,8192]{2,1,0:T(8,128)(2,1)S(1)} collective-permute-done((bf16[8,8,8192]{2,1,0:T(8,128)(2,1)S(1)}, bf16[8,8,8192]{2,1,0:T(8,128)(2,1)S(1)}, u32[]{:S(2)}, u32[]{:S(2)}) %collective-permute-start.3) | collective-permute-done | bytes 1048608 | tf_op jit(solution)/shard_map/ppermute | solution.py:16
  76.1 321.0 %while.15 = (s32[]{:T(128)}, f32[8,8192]{1,0:T(8,128)}, f32[8,128]{1,0:T(8,128)S(1)}, s32[13]{0:T(128)S(1)}, bf16[20,8960]{1,0:T(8,128)(2,1)}, /*index=5*/f32[8,...) while((s32[]{:T(128)}, f32[8,8192]{1,0:T(8,128)}, ...), condition=%wide.region_17.18_spmd.clone, body=%wide.region_3.17_spmd.clone.sunk | while | flops 3815698 | bytes 38420288 | solution.py:66
  79.7 1.3 slice_multiply_fusion.14
  98.4 2.4 fusion.285
  104.3 1.3 slice_multiply_fusion.14
  123.0 2.5 fusion.285
  129.0 1.3 slice_multiply_fusion.14
  147.7 2.5 fusion.285
  153.7 1.3 slice_multiply_fusion.14
  172.4 2.5 fusion.285
  178.4 1.3 slice_multiply_fusion.14
  197.1 2.5 fusion.285
  203.1 1.3 slice_multiply_fusion.14
  221.8 2.5 fusion.285
  227.8 1.3 slice_multiply_fusion.14
  246.4 2.5 fusion.285
  252.5 1.3 slice_multiply_fusion.14
  271.1 2.5 fusion.285
  277.2 1.3 slice_multiply_fusion.14
  295.8 2.5 fusion.285
  301.9 1.3 slice_multiply_fusion.14
  320.5 2.5 fusion.285
  326.6 1.3 slice_multiply_fusion.14
  345.2 2.5 fusion.285
  369.9 2.5 fusion.285
  394.6 2.5 fusion.285
  402.9 33.1 %all-reduce.30 = (f32[8]{0:T(128)S(1)}, f32[8]{0:T(128)S(1)}) all-reduce(f32[8]{0:T(128)S(1)} %get-tuple-element.221, f32[8]{0:T(128)S(1)} %get-tuple-element.220), channel_id=1, replica_groups=mesh['groups'=2,'col'=16] {'col'}, use_global_device_ids=true, to_apply=%region_20.21 | all-reduce | flops 16 | bytes 128 | tf_op jit(solution)/shard_map/psum | solution.py:108
  (1014 shorter events, 260.1 us)
Async XLA Ops:
  0.0 7.5 %copy-start.7 = (s32[8]{0:T(128)S(1)}, s32[8]{0:T(128)}, u32[]{:S(2)}) copy-start(s32[8]{0:T(128)} %param.9) | copy-start | bytes 100
  0.0 1.6 collective-permute-start
  2.7 9.6 %collective-permute-start.1 = (bf16[2,8,8192]{2,1,0:T(8,128)(2,1)S(1)}, bf16[2,8,8192]{2,1,0:T(8,128)(2,1)S(1)}, u32[]{:S(2)}, u32[]{:S(2)}) collective-permute-start(bf16[2,8,8192]{2,1,0:T(8,128)(2,1)S(1)} %maximum_select_fusion.3), channel_id=1, source_target_pairs={{0,2},{1,3},{2,0},{3,1},{4,6},{5,7},{6,4},{7,5},{8,10},{9,11},{10,... | collective-permute-start | bytes 786440 | tf_op jit(solution)/shard_map/ppermute | solution.py:16
  7.2 7.7 %copy-start.6 = (s32[1,8,128]{2,1,0:T(8,128)S(1)}, s32[1,8,128]{2,1,0:T(8,128)}, u32[]{:S(2)}) copy-start(s32[1,8,128]{2,1,0:T(8,128)} %param.10) | copy-start | bytes 12292
  12.3 16.3 %copy-start.3 = (bf16[1,8,8192]{2,1,0:T(8,128)(2,1)S(1)}, bf16[1,8,8192]{2,1,0:T(8,128)(2,1)}, u32[]{:S(2)}) copy-start(bf16[1,8,8192]{2,1,0:T(8,128)(2,1)} %param.7) | copy-start | bytes 393220
  12.3 13.5 %collective-permute-start.2 = (bf16[4,8,8192]{2,1,0:T(8,128)(2,1)S(1)}, bf16[4,8,8192]{2,1,0:T(8,128)(2,1)S(1)}, u32[]{:S(2)}, u32[]{:S(2)}) collective-permute-start(bf16[4,8,8192]{2,1,0:T(8,128)(2,1)S(1)} %maximum_select_fusion.2), channel_id=1, source_target_pairs={{0,4},{1,5},{2,6},{3,7},{4,0},{5,1},{6,2},{7,3},{8,12},{9,13},{10,... | collective-permute-start | bytes 1572872 | tf_op jit(solution)/shard_map/ppermute | solution.py:16
  26.0 47.2 %collective-permute-start.3 = (bf16[8,8,8192]{2,1,0:T(8,128)(2,1)S(1)}, bf16[8,8,8192]{2,1,0:T(8,128)(2,1)S(1)}, u32[]{:S(2)}, u32[]{:S(2)}) collective-permute-start(bf16[8,8,8192]{2,1,0:T(8,128)(2,1)S(1)} %maximum_select_fusion.1), channel_id=1, source_target_pairs={{0,8},{1,9},{2,10},{3,11},{4,12},{5,13},{6,14},{7,15},{8,0},{9,1},... | collective-permute-start | bytes 3145736 | tf_op jit(solution)/shard_map/ppermute | solution.py:16
  76.1 4.9 %copy-start = (f32[8,8192]{1,0:T(8,128)}, f32[8,8192]{1,0:T(8,128)S(1)}, u32[]{:S(2)}) copy-start(f32[8,8192]{1,0:T(8,128)S(1)} %get-tuple-element.456) | copy-start | bytes 786436 | tf_op jit(solution)/shard_map/while
  100.8 4.9 %copy-start = (f32[8,8192]{1,0:T(8,128)}, f32[8,8192]{1,0:T(8,128)S(1)}, u32[]{:S(2)}) copy-start(f32[8,8192]{1,0:T(8,128)S(1)} %get-tuple-element.456) | copy-start | bytes 786436 | tf_op jit(solution)/shard_map/while
  123.0 2.5 copy-start.1
  125.4 4.9 %copy-start = (f32[8,8192]{1,0:T(8,128)}, f32[8,8192]{1,0:T(8,128)S(1)}, u32[]{:S(2)}) copy-start(f32[8,8192]{1,0:T(8,128)S(1)} %get-tuple-element.456) | copy-start | bytes 786436 | tf_op jit(solution)/shard_map/while
  147.7 2.5 copy-start.1
  150.1 4.9 %copy-start = (f32[8,8192]{1,0:T(8,128)}, f32[8,8192]{1,0:T(8,128)S(1)}, u32[]{:S(2)}) copy-start(f32[8,8192]{1,0:T(8,128)S(1)} %get-tuple-element.456) | copy-start | bytes 786436 | tf_op jit(solution)/shard_map/while
  172.4 2.5 copy-start.1
  174.8 4.9 %copy-start = (f32[8,8192]{1,0:T(8,128)}, f32[8,8192]{1,0:T(8,128)S(1)}, u32[]{:S(2)}) copy-start(f32[8,8192]{1,0:T(8,128)S(1)} %get-tuple-element.456) | copy-start | bytes 786436 | tf_op jit(solution)/shard_map/while
  197.1 2.5 copy-start.1
  199.5 4.9 %copy-start = (f32[8,8192]{1,0:T(8,128)}, f32[8,8192]{1,0:T(8,128)S(1)}, u32[]{:S(2)}) copy-start(f32[8,8192]{1,0:T(8,128)S(1)} %get-tuple-element.456) | copy-start | bytes 786436 | tf_op jit(solution)/shard_map/while
  221.8 2.5 copy-start.1
  224.2 4.9 %copy-start = (f32[8,8192]{1,0:T(8,128)}, f32[8,8192]{1,0:T(8,128)S(1)}, u32[]{:S(2)}) copy-start(f32[8,8192]{1,0:T(8,128)S(1)} %get-tuple-element.456) | copy-start | bytes 786436 | tf_op jit(solution)/shard_map/while
  246.4 2.5 copy-start.1
  248.9 4.9 %copy-start = (f32[8,8192]{1,0:T(8,128)}, f32[8,8192]{1,0:T(8,128)S(1)}, u32[]{:S(2)}) copy-start(f32[8,8192]{1,0:T(8,128)S(1)} %get-tuple-element.456) | copy-start | bytes 786436 | tf_op jit(solution)/shard_map/while
  271.1 2.5 copy-start.1
  273.6 4.9 %copy-start = (f32[8,8192]{1,0:T(8,128)}, f32[8,8192]{1,0:T(8,128)S(1)}, u32[]{:S(2)}) copy-start(f32[8,8192]{1,0:T(8,128)S(1)} %get-tuple-element.456) | copy-start | bytes 786436 | tf_op jit(solution)/shard_map/while
  295.8 2.5 copy-start.1
  298.3 4.9 %copy-start = (f32[8,8192]{1,0:T(8,128)}, f32[8,8192]{1,0:T(8,128)S(1)}, u32[]{:S(2)}) copy-start(f32[8,8192]{1,0:T(8,128)S(1)} %get-tuple-element.456) | copy-start | bytes 786436 | tf_op jit(solution)/shard_map/while
  320.5 2.5 copy-start.1
  323.0 4.9 %copy-start = (f32[8,8192]{1,0:T(8,128)}, f32[8,8192]{1,0:T(8,128)S(1)}, u32[]{:S(2)}) copy-start(f32[8,8192]{1,0:T(8,128)S(1)} %get-tuple-element.456) | copy-start | bytes 786436 | tf_op jit(solution)/shard_map/while
  345.2 2.5 copy-start.1
  347.7 4.9 %copy-start = (f32[8,8192]{1,0:T(8,128)}, f32[8,8192]{1,0:T(8,128)S(1)}, u32[]{:S(2)}) copy-start(f32[8,8192]{1,0:T(8,128)S(1)} %get-tuple-element.456) | copy-start | bytes 786436 | tf_op jit(solution)/shard_map/while
  369.9 2.5 copy-start.1
  372.4 4.9 %copy-start = (f32[8,8192]{1,0:T(8,128)}, f32[8,8192]{1,0:T(8,128)S(1)}, u32[]{:S(2)}) copy-start(f32[8,8192]{1,0:T(8,128)S(1)} %get-tuple-element.456) | copy-start | bytes 786436 | tf_op jit(solution)/shard_map/while
  394.6 2.5 copy-start.1
  (4 other events, 5.3 us)
